TPU v7x, 32 devices: a whole 2x2x4 slice. The times are simulated.
32 devices in a mesh: gx: 8 (over y, x, core), gy: 4 (over z).
Axes of the slice: x: 2, y: 2, z: 4, core: 2. Of those that a mesh axis runs over, the one named last changes fastest.
Arguments:
- probe_signs: int32 [32, 16, 64, 128], P(None, 'gx', 'gy'), may hold values from 0 to 1
- diagonal: float32 [16, 64, 128], P('gx', 'gy'), may hold values from 0.25 to 4
Outputs:
- diagonal_blocks: float32 [3, 32, 32], replicated
- offdiag_blocks: float32 [3, 32, 32], replicated
- next_block: float32 [32, 16, 64, 128], P(None, 'gx', 'gy')
All inputs are finite; a program needn't handle non-finite values.
Results may differ from a plain program's by a relative error of at most 0.0006.
Values sent between devices are 32-bit elements; how exact they have to be, the bound alone decides.
A program may use at most 64 MiB of HBM per device.

v0:
```python
import jax
import jax.numpy as jnp
from jax import lax
from jax.sharding import PartitionSpec as P

ITERS = 3


def with_halo(block, sides, width):
    for axis, dim in sides:
        count = lax.axis_size(axis)
        forward = [(i, i + 1) for i in range(count - 1)]
        forward.append((count - 1, 0))
        backward = [(target, source) for source, target in forward]
        low = lax.ppermute(
            lax.slice_in_dim(block, block.shape[dim] - width, None, axis=dim), axis, forward
        )
        high = lax.ppermute(lax.slice_in_dim(block, 0, width, axis=dim), axis, backward)
        block = jnp.concatenate([low, block, high], axis=dim)
    return block


def stencil(vectors, diagonal):
    padded = with_halo(vectors, (("gx", 1), ("gy", 2)), 1)
    beside = padded[:, 2:, 1:-1] + padded[:, :-2, 1:-1] + padded[:, 1:-1, 2:] + padded[:, 1:-1, :-2]
    beside = beside + jnp.roll(vectors, 1, 3) + jnp.roll(vectors, -1, 3)
    return (6.0 + diagonal)[None] * vectors - beside


def inner_block(left, right):
    return jnp.einsum("pxyz,qxyz->pq", left, right, precision=lax.Precision.HIGHEST)


def combine(vectors, matrix):
    return jnp.einsum("pxyz,pq->qxyz", vectors, matrix, precision=lax.Precision.HIGHEST)


def small_product(left, right):
    return jnp.dot(left, right, precision=lax.Precision.HIGHEST)


def inverse_lower(gram_matrix):
    lower_factor = jnp.linalg.cholesky(gram_matrix)
    identity_matrix = jnp.eye(gram_matrix.shape[0], dtype=gram_matrix.dtype)
    inverse = lax.linalg.triangular_solve(lower_factor, identity_matrix, left_side=True, lower=True)
    return (lower_factor, inverse)


def per_device(probe_signs, diagonal):
    total_cells = (
        probe_signs.shape[1]
        * lax.axis_size("gx")
        * probe_signs.shape[2]
        * lax.axis_size("gy")
        * probe_signs.shape[3]
    )
    scale_factor = 1.0 / jnp.sqrt(jnp.float32(total_cells))
    probes = (2.0 * probe_signs.astype(jnp.float32) - 1.0) * scale_factor
    probe_matrix = lax.psum(inner_block(probes, probes), ("gx", "gy"))
    lower_factor, inverse = inverse_lower(probe_matrix)
    current = combine(probes, inverse.T)
    previous = None
    coupling = None
    alphas = []
    betas = []
    for iteration in range(ITERS):
        image = stencil(current, diagonal)
        if previous is not None:
            image = image - combine(previous, coupling)
        projected, image_gram = lax.psum(
            (inner_block(current, image), inner_block(image, image)), ("gx", "gy")
        )
        remain = image - combine(current, projected)
        remain_gram = image_gram - small_product(projected.T, projected)
        lower_factor, inverse = inverse_lower(remain_gram)
        alphas.append(projected)
        betas.append(lower_factor.T)
        previous = current
        coupling = lower_factor
        current = combine(remain, inverse.T)
    return (jnp.stack(alphas), jnp.stack(betas), current)


def solution(mesh):
    in_specs = (P(None, "gx", "gy", None), P("gx", "gy", None))
    out_specs = (P(), P(), P(None, "gx", "gy", None))
    return jax.shard_map(
        per_device, mesh=mesh, in_specs=in_specs, out_specs=out_specs, check_vma=False
    )
```

profile of v0, /device:TPU:14, one launch (start us, length us, event | category | flops | bytes accessed | tf_op | source)
XLA Modules:
  0.0 253.6 jit_solution(12887706050572880338)
XLA Ops:
  0.6 1.1 add_multiply_fusion
  1.8 0.8 convolution_bitcast_fusion.10
  2.6 40.3 %psum.49 = f32[32,32]{0,1:T(8,128)S(1)} all-reduce(f32[32,32]{0,1:T(8,128)S(1)} %convolution_bitcast_fusion.10), channel_id=1, replica_groups=mesh['gx'=8,'gy'=4] {'gx','gy'}, use_global_device_ids=true, to_apply=%region_0.0 | all-reduce | flops 1024 | bytes 8192 | tf_op jit(solution)/shard_map/psum | solution.py:59
  43.0 2.9 %cholesky.74 = f32[32,32]{1,0:T(8,128)S(1)} custom-call(f32[32,32]{1,0:T(8,128)S(1)} %fusion.38), custom_call_target="Cholesky" | custom-call | tf_op jit(solution)/shard_map/jit(cholesky)/cholesky | solution.py:43
  46.0 0.6 compare_reduce_fusion.3
  46.6 0.7 fusion.25
  47.3 2.4 custom-call.8
  49.9 0.9 fusion.18
  50.9 1.7 collective-permute-start
  53.1 3.7 %collective-permute-done.1 = f32[32,1,16,128]{3,0,2,1:T(8,128)S(1)} collective-permute-done((f32[32,1,16,128]{3,0,2,1:T(8,128)S(1)}, f32[32,1,16,128]{3,0,2,1:T(8,128)S(1)}, u32[]{:S(2)}, u32[]{:S(2)}) %collective-permute-start.1) | collective-permute-done | bytes 262176 | tf_op jit(solution)/shard_map/ppermute | solution.py:15
  56.8 0.9 collective-permute-done
  58.3 1.5 collective-permute-start.3
  59.8 2.2 collective-permute-done.2
  62.0 1.4 collective-permute-done.3
  65.0 44.6 %all-reduce.2 = (f32[32,32]{0,1:T(8,128)S(1)}, f32[32,32]{1,0:T(8,128)S(1)}) all-reduce(f32[32,32]{0,1:T(8,128)S(1)} %convolution_bitcast_fusion.7, f32[32,32]{1,0:T(8,128)S(1)} %convolution_bitcast_fusion.8), channel_id=1, replica_groups=mesh['gx'=8,'gy'=4] {'gx','gy'}, use_global_device_ids=true, to_apply=%region_4.7 | all-reduce | flops 2048 | bytes 16384 | tf_op jit(solution)/shard_map/psum | solution.py:70
  109.6 0.6 convolution_subtract_fusion.4
  110.5 2.9 %cholesky.85 = f32[32,32]{1,0:T(8,128)S(1)} custom-call(f32[32,32]{1,0:T(8,128)S(1)} %fusion.36), custom_call_target="Cholesky" | custom-call | tf_op jit(solution)/shard_map/jit(cholesky)/cholesky | solution.py:43
  113.5 0.6 compare_reduce_fusion.2
  114.1 0.7 fusion.40
  114.8 2.4 custom-call.9
  118.2 1.7 collective-permute-start.4
  120.1 5.4 %collective-permute-done.5 = f32[32,1,16,128]{3,0,2,1:T(8,128)S(1)} collective-permute-done((f32[32,1,16,128]{3,0,2,1:T(8,128)S(1)}, f32[32,1,16,128]{3,0,2,1:T(8,128)S(1)}, u32[]{:S(2)}, u32[]{:S(2)}) %collective-permute-start.5) | collective-permute-done | bytes 262176 | tf_op jit(solution)/shard_map/ppermute | solution.py:15
  125.6 2.0 collective-permute-start.7
  127.8 2.2 collective-permute-done.6
  130.1 0.8 collective-permute-done.7
  130.9 1.6 convolution_subtract_fusion.3
  133.6 42.3 %all-reduce.1 = (f32[32,32]{0,1:T(8,128)S(1)}, f32[32,32]{1,0:T(8,128)S(1)}) all-reduce(f32[32,32]{0,1:T(8,128)S(1)} %convolution_bitcast_fusion.4, f32[32,32]{1,0:T(8,128)S(1)} %convolution_bitcast_fusion.5), channel_id=1, replica_groups=mesh['gx'=8,'gy'=4] {'gx','gy'}, use_global_device_ids=true, to_apply=%region_6.9 | all-reduce | flops 2048 | bytes 16384 | tf_op jit(solution)/shard_map/psum | solution.py:70
  175.9 0.6 convolution_subtract_fusion.2
  176.8 2.9 %cholesky.96 = f32[32,32]{1,0:T(8,128)S(1)} custom-call(f32[32,32]{1,0:T(8,128)S(1)} %fusion.33), custom_call_target="Cholesky" | custom-call | tf_op jit(solution)/shard_map/jit(cholesky)/cholesky | solution.py:43
  179.8 0.6 compare_reduce_fusion.1
  180.4 0.7 fusion.41
  181.1 2.4 custom-call.10
  183.8 0.6 fusion.62
  184.4 1.7 collective-permute-start.8
  186.4 4.8 %collective-permute-done.9 = f32[32,1,16,128]{3,0,2,1:T(8,128)S(1)} collective-permute-done((f32[32,1,16,128]{3,0,2,1:T(8,128)S(1)}, f32[32,1,16,128]{3,0,2,1:T(8,128)S(1)}, u32[]{:S(2)}, u32[]{:S(2)}) %collective-permute-start.9) | collective-permute-done | bytes 262176 | tf_op jit(solution)/shard_map/ppermute | solution.py:15
  191.3 2.0 collective-permute-start.11
  193.5 2.0 collective-permute-done.10
  196.1 1.6 convolution_subtract_fusion.1
  198.7 44.0 %all-reduce = (f32[32,32]{1,0:T(8,128)S(1)}, f32[32,32]{0,1:T(8,128)S(1)}) all-reduce(f32[32,32]{1,0:T(8,128)S(1)} %convolution_bitcast_fusion.2, f32[32,32]{0,1:T(8,128)S(1)} %convolution_bitcast_fusion.1), channel_id=1, replica_groups=mesh['gx'=8,'gy'=4] {'gx','gy'}, use_global_device_ids=true, to_apply=%region_7.10 | all-reduce | flops 2048 | bytes 16384 | tf_op jit(solution)/shard_map/psum | solution.py:70
  242.7 0.6 convolution_subtract_fusion
  243.6 2.9 %cholesky.107 = f32[32,32]{1,0:T(8,128)S(1)} custom-call(f32[32,32]{1,0:T(8,128)S(1)} %fusion.30), custom_call_target="Cholesky" | custom-call | tf_op jit(solution)/shard_map/jit(cholesky)/cholesky | solution.py:43
  246.6 0.6 compare_reduce_fusion
  247.2 0.7 select_bitcast_fusion
  247.9 2.4 custom-call.11
  250.6 0.6 fusion.63
  251.2 1.1 copy.22
  252.3 0.7 copy.21
  253.0 0.6 pad_maximum_fusion.33
  (52 shorter events, 9.1 us)
Async XLA Ops:
  50.9 6.0 %collective-permute-start.1 = (f32[32,1,16,128]{3,0,2,1:T(8,128)S(1)}, f32[32,1,16,128]{3,0,2,1:T(8,128)S(1)}, u32[]{:S(2)}, u32[]{:S(2)}) collective-permute-start(f32[32,1,16,128]{3,0,2,1:T(8,128)S(1)} %get-tuple-element.36), channel_id=1, source_target_pairs={{0,4},{4,8},{8,12},{12,16},{16,20},{20,24},{24,28},{28,0},{1,5},{5... | collective-permute-start | bytes 786440 | tf_op jit(solution)/shard_map/ppermute | solution.py:15
  50.9 6.8 %collective-permute-start = (f32[32,1,16,128]{3,0,2,1:T(8,128)S(1)}, f32[32,1,16,128]{3,0,2,1:T(8,128)S(1)}, u32[]{:S(2)}, u32[]{:S(2)}) collective-permute-start(f32[32,1,16,128]{3,0,2,1:T(8,128)S(1)} %get-tuple-element.37), channel_id=1, source_target_pairs={{4,0},{8,4},{12,8},{16,12},{20,16},{24,20},{28,24},{0,28},{5,1},{9... | collective-permute-start | bytes 786440 | tf_op jit(solution)/shard_map/ppermute | solution.py:18
  53.1 6.7 %copy-start = (f32[2,16,128]{2,1,0:T(8,128)S(1)}, f32[2,16,128]{2,1,0:T(8,128)}, u32[]{:S(2)}) copy-start(f32[2,16,128]{2,1,0:T(8,128)} %param.6) | copy-start | bytes 49156
  57.7 4.3 %collective-permute-start.2 = (f32[32,4,1,128]{3,0,2,1:T(8,128)S(1)}, f32[32,4,1,128]{3,0,2,1:T(8,128)S(1)}, u32[]{:S(2)}, u32[]{:S(2)}) collective-permute-start(f32[32,4,1,128]{3,0,2,1:T(8,128)S(1)} %get-tuple-element.18), channel_id=1, source_target_pairs={{1,0},{2,1},{3,2},{0,3},{5,4},{6,5},{7,6},{4,7},{9,8},{10,9},{11,1... | collective-permute-start | bytes 196616 | tf_op jit(solution)/shard_map/ppermute | solution.py:18
  58.3 5.1 %collective-permute-start.3 = (f32[32,4,1,128]{3,0,2,1:T(8,128)S(1)}, f32[32,4,1,128]{3,0,2,1:T(8,128)S(1)}, u32[]{:S(2)}, u32[]{:S(2)}) collective-permute-start(f32[32,4,1,128]{3,0,2,1:T(8,128)S(1)} %get-tuple-element.19), channel_id=1, source_target_pairs={{0,1},{1,2},{2,3},{3,0},{4,5},{5,6},{6,7},{7,4},{8,9},{9,10},{10,1... | collective-permute-start | bytes 196616 | tf_op jit(solution)/shard_map/ppermute | solution.py:15
  118.1 7.4 %collective-permute-start.5 = (f32[32,1,16,128]{3,0,2,1:T(8,128)S(1)}, f32[32,1,16,128]{3,0,2,1:T(8,128)S(1)}, u32[]{:S(2)}, u32[]{:S(2)}) collective-permute-start(f32[32,1,16,128]{3,0,2,1:T(8,128)S(1)} %get-tuple-element.30), channel_id=1, source_target_pairs={{0,4},{4,8},{8,12},{12,16},{16,20},{20,24},{24,28},{28,0},{1,5},{5... | collective-permute-start | bytes 786440 | tf_op jit(solution)/shard_map/ppermute | solution.py:15
  118.2 7.4 %collective-permute-start.4 = (f32[32,1,16,128]{3,0,2,1:T(8,128)S(1)}, f32[32,1,16,128]{3,0,2,1:T(8,128)S(1)}, u32[]{:S(2)}, u32[]{:S(2)}) collective-permute-start(f32[32,1,16,128]{3,0,2,1:T(8,128)S(1)} %get-tuple-element.31), channel_id=1, source_target_pairs={{4,0},{8,4},{12,8},{16,12},{20,16},{24,20},{28,24},{0,28},{5,1},{9... | collective-permute-start | bytes 786440 | tf_op jit(solution)/shard_map/ppermute | solution.py:18
  125.5 4.5 %collective-permute-start.6 = (f32[32,4,1,128]{3,0,2,1:T(8,128)S(1)}, f32[32,4,1,128]{3,0,2,1:T(8,128)S(1)}, u32[]{:S(2)}, u32[]{:S(2)}) collective-permute-start(f32[32,4,1,128]{3,0,2,1:T(8,128)S(1)} %get-tuple-element.16), channel_id=1, source_target_pairs={{1,0},{2,1},{3,2},{0,3},{5,4},{6,5},{7,6},{4,7},{9,8},{10,9},{11,1... | collective-permute-start | bytes 196616 | tf_op jit(solution)/shard_map/ppermute | solution.py:18
  125.6 5.3 %collective-permute-start.7 = (f32[32,4,1,128]{3,0,2,1:T(8,128)S(1)}, f32[32,4,1,128]{3,0,2,1:T(8,128)S(1)}, u32[]{:S(2)}, u32[]{:S(2)}) collective-permute-start(f32[32,4,1,128]{3,0,2,1:T(8,128)S(1)} %get-tuple-element.17), channel_id=1, source_target_pairs={{0,1},{1,2},{2,3},{3,0},{4,5},{5,6},{6,7},{7,4},{8,9},{9,10},{10,1... | collective-permute-start | bytes 196616 | tf_op jit(solution)/shard_map/ppermute | solution.py:15
  184.4 6.8 %collective-permute-start.9 = (f32[32,1,16,128]{3,0,2,1:T(8,128)S(1)}, f32[32,1,16,128]{3,0,2,1:T(8,128)S(1)}, u32[]{:S(2)}, u32[]{:S(2)}) collective-permute-start(f32[32,1,16,128]{3,0,2,1:T(8,128)S(1)} %get-tuple-element.24), channel_id=1, source_target_pairs={{0,4},{4,8},{8,12},{12,16},{16,20},{20,24},{24,28},{28,0},{1,5},{5... | collective-permute-start | bytes 786440 | tf_op jit(solution)/shard_map/ppermute | solution.py:15
  184.4 6.8 %collective-permute-start.8 = (f32[32,1,16,128]{3,0,2,1:T(8,128)S(1)}, f32[32,1,16,128]{3,0,2,1:T(8,128)S(1)}, u32[]{:S(2)}, u32[]{:S(2)}) collective-permute-start(f32[32,1,16,128]{3,0,2,1:T(8,128)S(1)} %get-tuple-element.25), channel_id=1, source_target_pairs={{4,0},{8,4},{12,8},{16,12},{20,16},{24,20},{28,24},{0,28},{5,1},{9... | collective-permute-start | bytes 786440 | tf_op jit(solution)/shard_map/ppermute | solution.py:18
  191.2 4.3 %collective-permute-start.10 = (f32[32,4,1,128]{3,0,2,1:T(8,128)S(1)}, f32[32,4,1,128]{3,0,2,1:T(8,128)S(1)}, u32[]{:S(2)}, u32[]{:S(2)}) collective-permute-start(f32[32,4,1,128]{3,0,2,1:T(8,128)S(1)} %get-tuple-element.14), channel_id=1, source_target_pairs={{1,0},{2,1},{3,2},{0,3},{5,4},{6,5},{7,6},{4,7},{9,8},{10,9},{11,1... | collective-permute-start | bytes 196616 | tf_op jit(solution)/shard_map/ppermute | solution.py:18
  191.3 4.8 %collective-permute-start.11 = (f32[32,4,1,128]{3,0,2,1:T(8,128)S(1)}, f32[32,4,1,128]{3,0,2,1:T(8,128)S(1)}, u32[]{:S(2)}, u32[]{:S(2)}) collective-permute-start(f32[32,4,1,128]{3,0,2,1:T(8,128)S(1)} %get-tuple-element.15), channel_id=1, source_target_pairs={{0,1},{1,2},{2,3},{3,0},{4,5},{5,6},{6,7},{7,4},{8,9},{9,10},{10,1... | collective-permute-start | bytes 196616 | tf_op jit(solution)/shard_map/ppermute | solution.py:15
where the time goes:
time: 254 us
  blocking collectives  171 us (67%)
  other arithmetic  28.9 us (11%)
  waiting for transfers between devices  24.1 us (9%)
  matrix products  13.3 us (5%)
  starting transfers between devices  11.6 us (5%)
  local copies, waits for them, and re-layouts  3.44 us (1%)
    psum x3, blocking collectives, per_device(): lax.psum((inner_block(current, image), inner_block(image, image)), ('gx',...  131 us
    psum x1, blocking collectives, per_device(): probe_matrix = lax.psum(inner_block(probes, probes), ('gx', 'gy'))  40.3 us
    ppermute x6, waiting for transfers between devices, with_halo(): lax.ppermute(lax.slice_in_dim(block, block.shape[dim] - width, None, axis...  16.7 us
    another operation x12, other arithmetic, inverse_lower(): lower_factor = jnp.linalg.cholesky(gram_matrix)  14.4 us
    another operation x6, other arithmetic, inverse_lower(): lax.linalg.triangular_solve(lower_factor, identity_matrix, left_side=True...  11 us
    dot_general x9, matrix products, combine(): jnp.einsum('pxyz,pq->qxyz', vectors, matrix, precision=lax.Precision.HIGH...  7.62 us
    ppermute x6, waiting for transfers between devices, with_halo(): lax.ppermute(lax.slice_in_dim(block, 0, width, axis=dim), axis, backward)  7.37 us
    ppermute x6, starting transfers between devices, with_halo(): lax.ppermute(lax.slice_in_dim(block, 0, width, axis=dim), axis, backward)  5.89 us
  transfers between devices with their start and end apart: 12, of which 10 were waited for; matrix products, arithmetic and copies ran while one was open for 0% of the time, Pallas kernels for 0%

commit v1 on v0

--- a/solution.py
+++ b/solution.py
@@ -56,7 +56,9 @@
     )
     scale_factor = 1.0 / jnp.sqrt(jnp.float32(total_cells))
     probes = (2.0 * probe_signs.astype(jnp.float32) - 1.0) * scale_factor
-    probe_matrix = lax.psum(inner_block(probes, probes), ("gx", "gy"))
+    x = inner_block(probes, probes)
+    parts = lax.all_gather(x, ("gx", "gy"))
+    probe_matrix = jnp.sum(parts, axis=0)
     lower_factor, inverse = inverse_lower(probe_matrix)
     current = combine(probes, inverse.T)
     previous = None

time: 254 us -> 281 us (1.11)
  blocking collectives: 171 us -> 192 us
  starting transfers between devices: 11.6 us -> 14.7 us
    all_gather x0 -> x1, blocking collectives: none -> 61.2 us  [per_device(): parts = lax.all_gather(x, ('gx', 'gy'))]
    psum x1 -> x0, blocking collectives: 40.3 us -> none  [per_device(): probe_matrix = lax.psum(inner_block(probes, probes), ('gx', 'gy'))]
  transfers between devices with their start and end apart: 12 -> 12, of which waited for: 10 -> 11; matrix products, arithmetic and copies ran while one was open for 0% -> 0% of each run, Pallas kernels for 0% -> 0%
where the time goes in v1:
time: 281 us; the launch traced here: 280 us
  blocking collectives  192 us (68%)
  other arithmetic  29 us (10%)
  waiting for transfers between devices  26.7 us (10%)
  starting transfers between devices  14.7 us (5%)
  matrix products  13.3 us (5%)
  local copies, waits for them, and re-layouts  3.45 us (1%)
    psum x3, blocking collectives, per_device(): lax.psum((inner_block(current, image), inner_block(image, image)), ('gx',...  131 us
    all_gather x1, blocking collectives, per_device(): parts = lax.all_gather(x, ('gx', 'gy'))  61.2 us
    ppermute x6, waiting for transfers between devices, with_halo(): lax.ppermute(lax.slice_in_dim(block, block.shape[dim] - width, None, axis...  17 us
    another operation x12, other arithmetic, inverse_lower(): lower_factor = jnp.linalg.cholesky(gram_matrix)  14.4 us
    another operation x6, other arithmetic, inverse_lower(): lax.linalg.triangular_solve(lower_factor, identity_matrix, left_side=True...  11 us
    ppermute x6, waiting for transfers between devices, with_halo(): lax.ppermute(lax.slice_in_dim(block, 0, width, axis=dim), axis, backward)  9.69 us
    ppermute x6, starting transfers between devices, with_halo(): lax.ppermute(lax.slice_in_dim(block, 0, width, axis=dim), axis, backward)  8.46 us
    dot_general x9, matrix products, combine(): jnp.einsum('pxyz,pq->qxyz', vectors, matrix, precision=lax.Precision.HIGH...  7.62 us
  transfers between devices with their start and end apart: 12, of which 11 were waited for; matrix products, arithmetic and copies ran while one was open for 0% of the time, Pallas kernels for 0%

profile of v1, /device:TPU:14, one launch (start us, length us, event | category | flops | bytes accessed | tf_op | source)
XLA Modules:
  0.0 280.3 jit_solution(4371367451591645934)
XLA Ops:
  0.6 1.1 add_multiply_fusion
  1.8 0.8 convolution_bitcast_fusion.10
  2.6 61.2 %all-gather = f32[1024,32]{1,0:T(8,128)S(1)} all-gather(f32[32,32]{1,0:T(8,128)S(1)} %convolution_bitcast_fusion.10), channel_id=2, replica_groups=mesh['gx'=8,'gy'=4] {'gx','gy'}, dimensions={0}, use_global_device_ids=true | all-gather | bytes 135168 | tf_op jit(solution)/shard_map/all_gather | solution.py:60
  64.0 2.9 %cholesky.74 = f32[32,32]{1,0:T(8,128)S(1)} custom-call(f32[32,32]{1,0:T(8,128)S(1)} %fusion.38), custom_call_target="Cholesky" | custom-call | tf_op jit(solution)/shard_map/jit(cholesky)/cholesky | solution.py:43
  66.9 0.6 compare_reduce_fusion.3
  67.6 0.7 fusion.25
  68.2 2.4 custom-call.8
  70.9 0.9 fusion.18
  71.8 2.3 collective-permute-start.1
  74.5 3.1 %collective-permute-done.1 = f32[32,1,16,128]{3,0,2,1:T(8,128)S(1)} collective-permute-done((f32[32,1,16,128]{3,0,2,1:T(8,128)S(1)}, f32[32,1,16,128]{3,0,2,1:T(8,128)S(1)}, u32[]{:S(2)}, u32[]{:S(2)}) %collective-permute-start.1) | collective-permute-done | bytes 262176 | tf_op jit(solution)/shard_map/ppermute | solution.py:15
  77.7 2.8 %collective-permute-done = f32[32,1,16,128]{3,0,2,1:T(8,128)S(1)} collective-permute-done((f32[32,1,16,128]{3,0,2,1:T(8,128)S(1)}, f32[32,1,16,128]{3,0,2,1:T(8,128)S(1)}, u32[]{:S(2)}, u32[]{:S(2)}) %collective-permute-start) | collective-permute-done | bytes 262176 | tf_op jit(solution)/shard_map/ppermute | solution.py:18
  80.5 4.7 %collective-permute-start.2 = (f32[32,4,1,128]{3,0,2,1:T(8,128)S(1)}, f32[32,4,1,128]{3,0,2,1:T(8,128)S(1)}, u32[]{:S(2)}, u32[]{:S(2)}) collective-permute-start(f32[32,4,1,128]{3,0,2,1:T(8,128)S(1)} %get-tuple-element.21), channel_id=1, source_target_pairs={{1,0},{2,1},{3,2},{0,3},{5,4},{6,5},{7,6},{4,7},{9,8},{10,9},{11,1... | collective-permute-start | bytes 196616 | tf_op jit(solution)/shard_map/ppermute | solution.py:18
  85.2 1.9 collective-permute-done.2
  87.1 3.4 %collective-permute-done.3 = f32[32,4,1,128]{3,0,2,1:T(8,128)S(1)} collective-permute-done((f32[32,4,1,128]{3,0,2,1:T(8,128)S(1)}, f32[32,4,1,128]{3,0,2,1:T(8,128)S(1)}, u32[]{:S(2)}, u32[]{:S(2)}) %collective-permute-start.3) | collective-permute-done | bytes 65568 | tf_op jit(solution)/shard_map/ppermute | solution.py:15
  92.0 43.7 %all-reduce.2 = (f32[32,32]{0,1:T(8,128)S(1)}, f32[32,32]{1,0:T(8,128)S(1)}) all-reduce(f32[32,32]{0,1:T(8,128)S(1)} %convolution_bitcast_fusion.7, f32[32,32]{1,0:T(8,128)S(1)} %convolution_bitcast_fusion.8), channel_id=1, replica_groups=mesh['gx'=8,'gy'=4] {'gx','gy'}, use_global_device_ids=true, to_apply=%region_4.7 | all-reduce | flops 2048 | bytes 16384 | tf_op jit(solution)/shard_map/psum | solution.py:72
  135.8 0.6 convolution_subtract_fusion.4
  136.7 2.9 %cholesky.85 = f32[32,32]{1,0:T(8,128)S(1)} custom-call(f32[32,32]{1,0:T(8,128)S(1)} %fusion.36), custom_call_target="Cholesky" | custom-call | tf_op jit(solution)/shard_map/jit(cholesky)/cholesky | solution.py:43
  139.6 0.6 compare_reduce_fusion.2
  140.3 0.7 fusion.40
  140.9 2.4 custom-call.9
  143.6 0.6 fusion.61
  144.3 1.7 collective-permute-start.4
  146.3 4.1 %collective-permute-done.5 = f32[32,1,16,128]{3,0,2,1:T(8,128)S(1)} collective-permute-done((f32[32,1,16,128]{3,0,2,1:T(8,128)S(1)}, f32[32,1,16,128]{3,0,2,1:T(8,128)S(1)}, u32[]{:S(2)}, u32[]{:S(2)}) %collective-permute-start.5) | collective-permute-done | bytes 262176 | tf_op jit(solution)/shard_map/ppermute | solution.py:15
  150.3 0.6 collective-permute-done.4
  151.2 1.9 collective-permute-start.7
  153.3 2.0 collective-permute-done.6
  155.7 1.6 convolution_subtract_fusion.3
  158.4 44.8 %all-reduce.1 = (f32[32,32]{0,1:T(8,128)S(1)}, f32[32,32]{1,0:T(8,128)S(1)}) all-reduce(f32[32,32]{0,1:T(8,128)S(1)} %convolution_bitcast_fusion.4, f32[32,32]{1,0:T(8,128)S(1)} %convolution_bitcast_fusion.5), channel_id=1, replica_groups=mesh['gx'=8,'gy'=4] {'gx','gy'}, use_global_device_ids=true, to_apply=%region_6.9 | all-reduce | flops 2048 | bytes 16384 | tf_op jit(solution)/shard_map/psum | solution.py:72
  203.2 0.6 convolution_subtract_fusion.2
  204.2 2.9 %cholesky.96 = f32[32,32]{1,0:T(8,128)S(1)} custom-call(f32[32,32]{1,0:T(8,128)S(1)} %fusion.33), custom_call_target="Cholesky" | custom-call | tf_op jit(solution)/shard_map/jit(cholesky)/cholesky | solution.py:43
  207.1 0.6 compare_reduce_fusion.1
  207.8 0.7 fusion.41
  208.4 2.4 custom-call.10
  211.8 1.7 collective-permute-start.8
  213.7 5.4 %collective-permute-done.9 = f32[32,1,16,128]{3,0,2,1:T(8,128)S(1)} collective-permute-done((f32[32,1,16,128]{3,0,2,1:T(8,128)S(1)}, f32[32,1,16,128]{3,0,2,1:T(8,128)S(1)}, u32[]{:S(2)}, u32[]{:S(2)}) %collective-permute-start.9) | collective-permute-done | bytes 262176 | tf_op jit(solution)/shard_map/ppermute | solution.py:15
  219.2 2.0 collective-permute-start.11
  221.4 2.3 collective-permute-done.10
  223.7 0.6 collective-permute-done.11
  224.3 1.6 convolution_subtract_fusion.1
  227.0 42.4 %all-reduce = (f32[32,32]{1,0:T(8,128)S(1)}, f32[32,32]{0,1:T(8,128)S(1)}) all-reduce(f32[32,32]{1,0:T(8,128)S(1)} %convolution_bitcast_fusion.2, f32[32,32]{0,1:T(8,128)S(1)} %convolution_bitcast_fusion.1), channel_id=1, replica_groups=mesh['gx'=8,'gy'=4] {'gx','gy'}, use_global_device_ids=true, to_apply=%region_7.10 | all-reduce | flops 2048 | bytes 16384 | tf_op jit(solution)/shard_map/psum | solution.py:72
  269.4 0.6 convolution_subtract_fusion
  270.4 2.9 %cholesky.107 = f32[32,32]{1,0:T(8,128)S(1)} custom-call(f32[32,32]{1,0:T(8,128)S(1)} %fusion.30), custom_call_target="Cholesky" | custom-call | tf_op jit(solution)/shard_map/jit(cholesky)/cholesky | solution.py:43
  273.3 0.6 compare_reduce_fusion
  274.0 0.7 select_bitcast_fusion
  274.6 2.4 custom-call.11
  277.9 1.1 copy.38
  279.0 0.7 copy.37
  279.7 0.6 pad_maximum_fusion.33
  (53 shorter events, 9.1 us)
Async XLA Ops:
  71.8 5.8 %collective-permute-start.1 = (f32[32,1,16,128]{3,0,2,1:T(8,128)S(1)}, f32[32,1,16,128]{3,0,2,1:T(8,128)S(1)}, u32[]{:S(2)}, u32[]{:S(2)}) collective-permute-start(f32[32,1,16,128]{3,0,2,1:T(8,128)S(1)} %get-tuple-element.39), channel_id=1, source_target_pairs={{0,4},{4,8},{8,12},{12,16},{16,20},{20,24},{24,28},{28,0},{1,5},{5... | collective-permute-start | bytes 786440 | tf_op jit(solution)/shard_map/ppermute | solution.py:15
  74.1 6.4 %collective-permute-start = (f32[32,1,16,128]{3,0,2,1:T(8,128)S(1)}, f32[32,1,16,128]{3,0,2,1:T(8,128)S(1)}, u32[]{:S(2)}, u32[]{:S(2)}) collective-permute-start(f32[32,1,16,128]{3,0,2,1:T(8,128)S(1)} %get-tuple-element.40), channel_id=1, source_target_pairs={{4,0},{8,4},{12,8},{16,12},{20,16},{24,20},{28,24},{0,28},{5,1},{9... | collective-permute-start | bytes 786440 | tf_op jit(solution)/shard_map/ppermute | solution.py:18
  74.5 10.7 %copy-start = (f32[2,16,128]{2,1,0:T(8,128)S(1)}, f32[2,16,128]{2,1,0:T(8,128)}, u32[]{:S(2)}) copy-start(f32[2,16,128]{2,1,0:T(8,128)} %param.6) | copy-start | bytes 49156
  80.5 6.6 %collective-permute-start.2 = (f32[32,4,1,128]{3,0,2,1:T(8,128)S(1)}, f32[32,4,1,128]{3,0,2,1:T(8,128)S(1)}, u32[]{:S(2)}, u32[]{:S(2)}) collective-permute-start(f32[32,4,1,128]{3,0,2,1:T(8,128)S(1)} %get-tuple-element.21), channel_id=1, source_target_pairs={{1,0},{2,1},{3,2},{0,3},{5,4},{6,5},{7,6},{4,7},{9,8},{10,9},{11,1... | collective-permute-start | bytes 196616 | tf_op jit(solution)/shard_map/ppermute | solution.py:18
  85.2 5.3 %collective-permute-start.3 = (f32[32,4,1,128]{3,0,2,1:T(8,128)S(1)}, f32[32,4,1,128]{3,0,2,1:T(8,128)S(1)}, u32[]{:S(2)}, u32[]{:S(2)}) collective-permute-start(f32[32,4,1,128]{3,0,2,1:T(8,128)S(1)} %get-tuple-element.22), channel_id=1, source_target_pairs={{0,1},{1,2},{2,3},{3,0},{4,5},{5,6},{6,7},{7,4},{8,9},{9,10},{10,1... | collective-permute-start | bytes 196616 | tf_op jit(solution)/shard_map/ppermute | solution.py:15
  144.3 6.1 %collective-permute-start.5 = (f32[32,1,16,128]{3,0,2,1:T(8,128)S(1)}, f32[32,1,16,128]{3,0,2,1:T(8,128)S(1)}, u32[]{:S(2)}, u32[]{:S(2)}) collective-permute-start(f32[32,1,16,128]{3,0,2,1:T(8,128)S(1)} %get-tuple-element.33), channel_id=1, source_target_pairs={{0,4},{4,8},{8,12},{12,16},{16,20},{20,24},{24,28},{28,0},{1,5},{5... | collective-permute-start | bytes 786440 | tf_op jit(solution)/shard_map/ppermute | solution.py:15
  144.3 6.7 %collective-permute-start.4 = (f32[32,1,16,128]{3,0,2,1:T(8,128)S(1)}, f32[32,1,16,128]{3,0,2,1:T(8,128)S(1)}, u32[]{:S(2)}, u32[]{:S(2)}) collective-permute-start(f32[32,1,16,128]{3,0,2,1:T(8,128)S(1)} %get-tuple-element.34), channel_id=1, source_target_pairs={{4,0},{8,4},{12,8},{16,12},{20,16},{24,20},{28,24},{0,28},{5,1},{9... | collective-permute-start | bytes 786440 | tf_op jit(solution)/shard_map/ppermute | solution.py:18
  151.0 4.3 %collective-permute-start.6 = (f32[32,4,1,128]{3,0,2,1:T(8,128)S(1)}, f32[32,4,1,128]{3,0,2,1:T(8,128)S(1)}, u32[]{:S(2)}, u32[]{:S(2)}) collective-permute-start(f32[32,4,1,128]{3,0,2,1:T(8,128)S(1)} %get-tuple-element.19), channel_id=1, source_target_pairs={{1,0},{2,1},{3,2},{0,3},{5,4},{6,5},{7,6},{4,7},{9,8},{10,9},{11,1... | collective-permute-start | bytes 196616 | tf_op jit(solution)/shard_map/ppermute | solution.py:18
  151.2 4.5 %collective-permute-start.7 = (f32[32,4,1,128]{3,0,2,1:T(8,128)S(1)}, f32[32,4,1,128]{3,0,2,1:T(8,128)S(1)}, u32[]{:S(2)}, u32[]{:S(2)}) collective-permute-start(f32[32,4,1,128]{3,0,2,1:T(8,128)S(1)} %get-tuple-element.20), channel_id=1, source_target_pairs={{0,1},{1,2},{2,3},{3,0},{4,5},{5,6},{6,7},{7,4},{8,9},{9,10},{10,1... | collective-permute-start | bytes 196616 | tf_op jit(solution)/shard_map/ppermute | solution.py:15
  211.7 7.4 %collective-permute-start.9 = (f32[32,1,16,128]{3,0,2,1:T(8,128)S(1)}, f32[32,1,16,128]{3,0,2,1:T(8,128)S(1)}, u32[]{:S(2)}, u32[]{:S(2)}) collective-permute-start(f32[32,1,16,128]{3,0,2,1:T(8,128)S(1)} %get-tuple-element.27), channel_id=1, source_target_pairs={{0,4},{4,8},{8,12},{12,16},{16,20},{20,24},{24,28},{28,0},{1,5},{5... | collective-permute-start | bytes 786440 | tf_op jit(solution)/shard_map/ppermute | solution.py:15
  211.8 7.3 %collective-permute-start.8 = (f32[32,1,16,128]{3,0,2,1:T(8,128)S(1)}, f32[32,1,16,128]{3,0,2,1:T(8,128)S(1)}, u32[]{:S(2)}, u32[]{:S(2)}) collective-permute-start(f32[32,1,16,128]{3,0,2,1:T(8,128)S(1)} %get-tuple-element.28), channel_id=1, source_target_pairs={{4,0},{8,4},{12,8},{16,12},{20,16},{24,20},{28,24},{0,28},{5,1},{9... | collective-permute-start | bytes 786440 | tf_op jit(solution)/shard_map/ppermute | solution.py:18
  219.1 4.6 %collective-permute-start.10 = (f32[32,4,1,128]{3,0,2,1:T(8,128)S(1)}, f32[32,4,1,128]{3,0,2,1:T(8,128)S(1)}, u32[]{:S(2)}, u32[]{:S(2)}) collective-permute-start(f32[32,4,1,128]{3,0,2,1:T(8,128)S(1)} %get-tuple-element.17), channel_id=1, source_target_pairs={{1,0},{2,1},{3,2},{0,3},{5,4},{6,5},{7,6},{4,7},{9,8},{10,9},{11,1... | collective-permute-start | bytes 196616 | tf_op jit(solution)/shard_map/ppermute | solution.py:18
  219.2 5.1 %collective-permute-start.11 = (f32[32,4,1,128]{3,0,2,1:T(8,128)S(1)}, f32[32,4,1,128]{3,0,2,1:T(8,128)S(1)}, u32[]{:S(2)}, u32[]{:S(2)}) collective-permute-start(f32[32,4,1,128]{3,0,2,1:T(8,128)S(1)} %get-tuple-element.18), channel_id=1, source_target_pairs={{0,1},{1,2},{2,3},{3,0},{4,5},{5,6},{6,7},{7,4},{8,9},{9,10},{10,1... | collective-permute-start | bytes 196616 | tf_op jit(solution)/shard_map/ppermute | solution.py:15
